TPU v7x, 256 devices: a whole 4x4x8 slice. The times are simulated.
256 devices in a mesh: shot: 16 (over x_lo, z), rcv: 8 (over y, x_hi), surf: 2 (over core).
Axes of the slice: x: 4 (x_hi: 2, x_lo: 2; x = x_hi * 2 + x_lo), y: 4, z: 8, core: 2. Of those that a mesh axis runs over, the one named last changes fastest.
Arguments:
- traces: bfloat16 [2, 16384, 256], P('surf', 'shot'), may hold values from -6 to 6
- trace_block: int32 [2, 16384, 1], P('surf', 'shot'), may hold values from 0 to 15; in each aligned block of 128 rows (0 to 127, 128 to 255, ..., all dimensions but the last counted through in order) at most 16 rows name the same one
- trace_shot: int32 [2, 16384], P('surf', 'shot'), may hold values from 0 to 15
- trace_point: int32 [2, 16384], P('surf', 'shot'), may hold values from 0 to 255
- recv_panel: bfloat16 [129, 2, 512, 1024], P(None, None, ('shot', 'surf'), 'rcv'), may hold values from -0.375 to 0.375
Outputs:
- multiples: bfloat16 [129, 2, 256, 1024], P(None, None, ('shot', 'surf'), 'rcv')
Inputs may be any that keep to these rules, and one draw needn't show every extreme that they name: `trace_block`: in each aligned block of 128 rows, at most 16 rows name one shot block.
All inputs are finite; a program needn't handle non-finite values.
Results may differ from a plain program's by a relative error of at most 0.012.
Values may be sent and summed in bfloat16 or wider, within the bound.
A program may use at most 64 MiB of HBM per device.

v0:
```python
import math
import jax
import jax.numpy as jnp
from jax import lax
from jax.sharding import PartitionSpec as P

SHOTS_PER_INDEX = 16


def split_up(array, dim, size):
    before, after = (array.shape[:dim], array.shape[dim + 1 :])
    return jnp.moveaxis(array.reshape(*before, size, -1, *after), dim, 0)


def summed_on_arrival(array, axis, dim):
    size = lax.axis_size(axis)
    parts = lax.all_to_all(split_up(array, dim, size), axis, 0, 0, tiled=True)
    return jnp.sum(parts.astype(jnp.float32), axis=0)


def transform_rows(samples, window_len, bin_count):
    sample_index = lax.broadcasted_iota(jnp.int32, (window_len, bin_count), 0)
    freq_index = lax.broadcasted_iota(jnp.int32, (window_len, bin_count), 1)
    phase_angle = (sample_index * freq_index % window_len).astype(jnp.float32) * (
        2.0 * math.pi / window_len
    )
    norm_factor = 1.0 / math.sqrt(window_len)
    table = jnp.concatenate(
        [jnp.cos(phase_angle) * norm_factor, -jnp.sin(phase_angle) * norm_factor], axis=1
    )
    table_high = table.astype(jnp.bfloat16)
    table_low = (table - table_high.astype(jnp.float32)).astype(jnp.bfloat16)
    result = jnp.dot(samples, table_high, preferred_element_type=jnp.float32)
    result = result + jnp.dot(samples, table_low, preferred_element_type=jnp.float32)
    real_part = result[:, :bin_count]
    imag_part = result[:, bin_count:]
    return jnp.stack([real_part, imag_part], axis=1).astype(jnp.bfloat16)


def route_rows(spectra, owners, targets, places, owner_count, empty_id):
    row_count = owners.shape[0]
    owner_hit = owners[:, None] == lax.broadcasted_iota(jnp.int32, (1, owner_count), 1)
    earlier = lax.broadcasted_iota(jnp.int32, (row_count, row_count), 0) > lax.broadcasted_iota(
        jnp.int32, (row_count, row_count), 1
    )
    before = jnp.dot(
        earlier.astype(jnp.bfloat16),
        owner_hit.astype(jnp.bfloat16),
        preferred_element_type=jnp.float32,
    )
    slot_rank = jnp.sum(jnp.where(owner_hit, before, 0.0), axis=1).astype(jnp.int32)
    position = owners * places + slot_rank
    slot_total = owner_count * places
    slot_hit = position[:, None] == lax.broadcasted_iota(jnp.int32, (1, slot_total), 1)
    flat_spectra = spectra.reshape(row_count, -1)
    buffer = lax.dot_general(
        slot_hit.astype(jnp.bfloat16),
        flat_spectra,
        (((0,), (0,)), ((), ())),
        preferred_element_type=jnp.float32,
    )
    buffer = buffer.astype(spectra.dtype)
    labels = jnp.max(jnp.where(slot_hit, targets[:, None], -1), axis=0)
    labels = jnp.where(labels < 0, empty_id, labels)
    return (
        buffer.reshape((owner_count, places) + spectra.shape[1:]),
        labels.reshape(owner_count, places),
    )


def bin_panel(received, labels, shot_rows, point_count):
    freq_count = received.shape[-1]
    flat_rows = received.reshape(-1, 2 * freq_count)
    flat_labels = labels.reshape(-1)
    point_iota = lax.broadcasted_iota(jnp.int32, (1, point_count), 1)

    def one_shot(shot_id):
        local_label = flat_labels - shot_id * point_count
        point_hit = local_label[:, None] == point_iota
        totals = lax.dot_general(
            point_hit.astype(jnp.bfloat16),
            flat_rows,
            (((0,), (0,)), ((), ())),
            preferred_element_type=jnp.float32,
        )
        coverage = jnp.sum(point_hit.astype(jnp.float32), axis=0)
        return (totals / jnp.maximum(coverage, 1.0)[:, None]).astype(jnp.bfloat16)

    panel = lax.map(one_shot, jnp.arange(shot_rows, dtype=jnp.int32))
    return panel.reshape(shot_rows, point_count, 2, freq_count).transpose(3, 2, 0, 1)


def product(left_edge, right_edge):
    return jnp.einsum("bhv,bvy->bhy", left_edge, right_edge, preferred_element_type=jnp.float32)


def local(traces, trace_block, trace_shot, trace_point, recv_panel):
    shot_count = lax.axis_size("shot")
    rcv_count = lax.axis_size("rcv")
    freq_count = recv_panel.shape[0]
    half_points = recv_panel.shape[2] * shot_count
    window_len = traces.shape[2]
    row_count = traces.shape[1]
    part_rows = row_count // rcv_count
    capacity = 2 * part_rows // shot_count
    empty_id = SHOTS_PER_INDEX * half_points
    samples = traces[0]
    owners = trace_block[0, :, 0]
    targets = trace_shot[0] * half_points + trace_point[0]
    spectra = transform_rows(samples, window_len, freq_count)
    buffer, labels = route_rows(
        spectra, owners, targets, rcv_count * capacity, shot_count, empty_id
    )
    received, got_labels = (
        lax.all_to_all(buffer, "shot", split_axis=0, concat_axis=0, tiled=True),
        lax.all_to_all(labels, "shot", split_axis=0, concat_axis=0, tiled=True),
    )
    panel = bin_panel(received, got_labels, SHOTS_PER_INDEX, half_points)
    receiver = lax.all_gather(recv_panel, "shot", axis=2, tiled=True)
    real_part = product(panel[:, 0], receiver[:, 0]) - product(panel[:, 1], receiver[:, 1])
    imag_part = product(panel[:, 0], receiver[:, 1]) + product(panel[:, 1], receiver[:, 0])
    partial_value = jnp.stack([real_part, imag_part], axis=1)
    half_term = lax.optimization_barrier(partial_value.astype(jnp.bfloat16)).astype(jnp.float32)
    result = summed_on_arrival(half_term.astype(jnp.bfloat16), "surf", 2)
    return result.astype(jnp.bfloat16)


def solution(mesh):
    in_specs = (
        P("surf", "shot", None),
        P("surf", "shot", None),
        P("surf", "shot"),
        P("surf", "shot"),
        P(None, None, ("shot", "surf"), "rcv"),
    )
    out_specs = P(None, None, ("shot", "surf"), "rcv")
    return jax.shard_map(local, mesh=mesh, in_specs=in_specs, out_specs=out_specs, check_vma=False)
```

profile of v0, /device:TPU:23, one launch (start us, length us, event | category | flops | bytes accessed | tf_op | source)
XLA Modules:
  0.0 263.6 jit_solution(1235971979130966523)
XLA Ops:
  6.5 2.4 copy.40
  11.5 1.8 fusion.17
  13.8 1.8 copy.36
  15.5 9.4 %all-to-all-start.1 = ((bf16[16,128,2,129]{1,2,3,0:T(2,128)(2,1)}), bf16[16,128,2,129]{1,2,3,0:T(2,128)(2,1)S(1)}, u32[]{:S(2)}, u32[]{:S(2)}) async-start(bf16[16,128,2,129]{1,2,3,0:T(2,128)(2,1)} %copy.36), calls=%async_computation.1 | async-start | bytes 2113536 | tf_op jit(solution)/shard_map/all_to_all | solution.py:115
  25.0 1.6 select_reduce_fusion
  26.6 0.6 compare_select_fusion
  27.2 33.8 %all-to-all-done.1 = bf16[16,128,2,129]{1,2,3,0:T(2,128)(2,1)S(1)} async-done(((bf16[16,128,2,129]{1,2,3,0:T(2,128)(2,1)}), bf16[16,128,2,129]{1,2,3,0:T(2,128)(2,1)S(1)}, u32[]{:S(2)}, u32[]{:S(2)}) %all-to-all-start.1) | async-done | bytes 1056800 | tf_op jit(solution)/shard_map/all_to_all | solution.py:115
  61.0 5.1 %all-to-all-start = ((s32[16,1,128]{2,1,0:T(1,128)}), s32[16,1,128]{2,1,0:T(1,128)S(1)}, u32[]{:S(2)}, u32[]{:S(2)}) async-start(s32[16,1,128]{2,1,0:T(1,128)} %compare_select_fusion), calls=%async_computation | async-start | bytes 16384 | tf_op jit(solution)/shard_map/all_to_all | solution.py:116
  66.1 8.1 %copy.44 = bf16[16,128,2,129]{3,2,1,0:T(2,128)(2,1)S(1)} copy(bf16[16,128,2,129]{1,2,3,0:T(2,128)(2,1)} %copy-done.2) | data formatting | bytes 2113536
  74.2 2.0 reshape.78
  76.2 74.6 %while.11 = (s32[]{:T(128)}, bf16[16,256,258]{1,2,0:T(8,128)(2,1)}, s32[16]{0:T(128)S(1)}, s32[2048]{0:T(1024)S(1)}, bf16[2048,258]{1,0:T(8,128)(2,1)}, /*index=5*/s32[]{:T(128)}, s32[1]{0:T(128)}) while((s32[]{:T(128)}, bf16[16,256,258]{1,2,0:T(8,128)(2,1)}, s32[16]{0:T(128)S(1)}, s32[2048]{0:T(1024)S(1)}, ...), condition=%wide.region_4.5_spmd.clone, body=%wide.region_2.4_spmd.clone.sunk | while | flops 272763904 | bytes 1745513 | solution.py:89
  76.2 0.6 dynamic_slice.6
  77.8 3.1 %fusion.50 = bf16[16,256,258]{1,2,0:T(8,128)(2,1)} fusion(bf16[16,256,258]{1,2,0:T(8,128)(2,1)} %get-tuple-element.128, s32[]{:T(128)} %get-tuple-element.127, bf16[2048,258]{1,0:T(8,128)(2,1)} %get-tuple-element.138, s32[2048]{0:T(1024)S(1)} %broadcast_subtract_fusion.2, f32[256]{0:T(256)S(1)} %broadcast_maximum_fusion.2), kind=kOutput, calls=%fused_computation.8.clone.1 | convolution fusion | flops 271188992 | bytes 1717760 | tf_op jit(solution)/shard_map/while/body/eval_jaxpr/dot_general | solution.py:80
  80.9 0.6 dynamic_slice.6
  82.5 3.0 %fusion.50 = bf16[16,256,258]{1,2,0:T(8,128)(2,1)} fusion(bf16[16,256,258]{1,2,0:T(8,128)(2,1)} %get-tuple-element.128, s32[]{:T(128)} %get-tuple-element.127, bf16[2048,258]{1,0:T(8,128)(2,1)} %get-tuple-element.138, s32[2048]{0:T(1024)S(1)} %broadcast_subtract_fusion.2, f32[256]{0:T(256)S(1)} %broadcast_maximum_fusion.2), kind=kOutput, calls=%fused_computation.8.clone.1 | convolution fusion | flops 271188992 | bytes 1717760 | tf_op jit(solution)/shard_map/while/body/eval_jaxpr/dot_general | solution.py:80
  85.6 0.6 dynamic_slice.6
  87.2 3.1 %fusion.50 = bf16[16,256,258]{1,2,0:T(8,128)(2,1)} fusion(bf16[16,256,258]{1,2,0:T(8,128)(2,1)} %get-tuple-element.128, s32[]{:T(128)} %get-tuple-element.127, bf16[2048,258]{1,0:T(8,128)(2,1)} %get-tuple-element.138, s32[2048]{0:T(1024)S(1)} %broadcast_subtract_fusion.2, f32[256]{0:T(256)S(1)} %broadcast_maximum_fusion.2), kind=kOutput, calls=%fused_computation.8.clone.1 | convolution fusion | flops 271188992 | bytes 1717760 | tf_op jit(solution)/shard_map/while/body/eval_jaxpr/dot_general | solution.py:80
  90.2 0.6 dynamic_slice.6
  91.8 3.0 %fusion.50 = bf16[16,256,258]{1,2,0:T(8,128)(2,1)} fusion(bf16[16,256,258]{1,2,0:T(8,128)(2,1)} %get-tuple-element.128, s32[]{:T(128)} %get-tuple-element.127, bf16[2048,258]{1,0:T(8,128)(2,1)} %get-tuple-element.138, s32[2048]{0:T(1024)S(1)} %broadcast_subtract_fusion.2, f32[256]{0:T(256)S(1)} %broadcast_maximum_fusion.2), kind=kOutput, calls=%fused_computation.8.clone.1 | convolution fusion | flops 271188992 | bytes 1717760 | tf_op jit(solution)/shard_map/while/body/eval_jaxpr/dot_general | solution.py:80
  94.9 0.6 dynamic_slice.6
  96.5 3.1 %fusion.50 = bf16[16,256,258]{1,2,0:T(8,128)(2,1)} fusion(bf16[16,256,258]{1,2,0:T(8,128)(2,1)} %get-tuple-element.128, s32[]{:T(128)} %get-tuple-element.127, bf16[2048,258]{1,0:T(8,128)(2,1)} %get-tuple-element.138, s32[2048]{0:T(1024)S(1)} %broadcast_subtract_fusion.2, f32[256]{0:T(256)S(1)} %broadcast_maximum_fusion.2), kind=kOutput, calls=%fused_computation.8.clone.1 | convolution fusion | flops 271188992 | bytes 1717760 | tf_op jit(solution)/shard_map/while/body/eval_jaxpr/dot_general | solution.py:80
  99.5 0.6 dynamic_slice.6
  101.1 3.0 %fusion.50 = bf16[16,256,258]{1,2,0:T(8,128)(2,1)} fusion(bf16[16,256,258]{1,2,0:T(8,128)(2,1)} %get-tuple-element.128, s32[]{:T(128)} %get-tuple-element.127, bf16[2048,258]{1,0:T(8,128)(2,1)} %get-tuple-element.138, s32[2048]{0:T(1024)S(1)} %broadcast_subtract_fusion.2, f32[256]{0:T(256)S(1)} %broadcast_maximum_fusion.2), kind=kOutput, calls=%fused_computation.8.clone.1 | convolution fusion | flops 271188992 | bytes 1717760 | tf_op jit(solution)/shard_map/while/body/eval_jaxpr/dot_general | solution.py:80
  104.2 0.6 dynamic_slice.6
  105.8 3.0 %fusion.50 = bf16[16,256,258]{1,2,0:T(8,128)(2,1)} fusion(bf16[16,256,258]{1,2,0:T(8,128)(2,1)} %get-tuple-element.128, s32[]{:T(128)} %get-tuple-element.127, bf16[2048,258]{1,0:T(8,128)(2,1)} %get-tuple-element.138, s32[2048]{0:T(1024)S(1)} %broadcast_subtract_fusion.2, f32[256]{0:T(256)S(1)} %broadcast_maximum_fusion.2), kind=kOutput, calls=%fused_computation.8.clone.1 | convolution fusion | flops 271188992 | bytes 1717760 | tf_op jit(solution)/shard_map/while/body/eval_jaxpr/dot_general | solution.py:80
  108.8 0.6 dynamic_slice.6
  110.5 3.1 %fusion.50 = bf16[16,256,258]{1,2,0:T(8,128)(2,1)} fusion(bf16[16,256,258]{1,2,0:T(8,128)(2,1)} %get-tuple-element.128, s32[]{:T(128)} %get-tuple-element.127, bf16[2048,258]{1,0:T(8,128)(2,1)} %get-tuple-element.138, s32[2048]{0:T(1024)S(1)} %broadcast_subtract_fusion.2, f32[256]{0:T(256)S(1)} %broadcast_maximum_fusion.2), kind=kOutput, calls=%fused_computation.8.clone.1 | convolution fusion | flops 271188992 | bytes 1717760 | tf_op jit(solution)/shard_map/while/body/eval_jaxpr/dot_general | solution.py:80
  113.5 0.6 dynamic_slice.6
  115.1 3.0 %fusion.50 = bf16[16,256,258]{1,2,0:T(8,128)(2,1)} fusion(bf16[16,256,258]{1,2,0:T(8,128)(2,1)} %get-tuple-element.128, s32[]{:T(128)} %get-tuple-element.127, bf16[2048,258]{1,0:T(8,128)(2,1)} %get-tuple-element.138, s32[2048]{0:T(1024)S(1)} %broadcast_subtract_fusion.2, f32[256]{0:T(256)S(1)} %broadcast_maximum_fusion.2), kind=kOutput, calls=%fused_computation.8.clone.1 | convolution fusion | flops 271188992 | bytes 1717760 | tf_op jit(solution)/shard_map/while/body/eval_jaxpr/dot_general | solution.py:80
  118.2 0.6 dynamic_slice.6
  119.8 3.1 %fusion.50 = bf16[16,256,258]{1,2,0:T(8,128)(2,1)} fusion(bf16[16,256,258]{1,2,0:T(8,128)(2,1)} %get-tuple-element.128, s32[]{:T(128)} %get-tuple-element.127, bf16[2048,258]{1,0:T(8,128)(2,1)} %get-tuple-element.138, s32[2048]{0:T(1024)S(1)} %broadcast_subtract_fusion.2, f32[256]{0:T(256)S(1)} %broadcast_maximum_fusion.2), kind=kOutput, calls=%fused_computation.8.clone.1 | convolution fusion | flops 271188992 | bytes 1717760 | tf_op jit(solution)/shard_map/while/body/eval_jaxpr/dot_general | solution.py:80
  122.9 0.6 dynamic_slice.6
  124.5 3.0 %fusion.50 = bf16[16,256,258]{1,2,0:T(8,128)(2,1)} fusion(bf16[16,256,258]{1,2,0:T(8,128)(2,1)} %get-tuple-element.128, s32[]{:T(128)} %get-tuple-element.127, bf16[2048,258]{1,0:T(8,128)(2,1)} %get-tuple-element.138, s32[2048]{0:T(1024)S(1)} %broadcast_subtract_fusion.2, f32[256]{0:T(256)S(1)} %broadcast_maximum_fusion.2), kind=kOutput, calls=%fused_computation.8.clone.1 | convolution fusion | flops 271188992 | bytes 1717760 | tf_op jit(solution)/shard_map/while/body/eval_jaxpr/dot_general | solution.py:80
  127.5 0.6 dynamic_slice.6
  129.1 3.1 %fusion.50 = bf16[16,256,258]{1,2,0:T(8,128)(2,1)} fusion(bf16[16,256,258]{1,2,0:T(8,128)(2,1)} %get-tuple-element.128, s32[]{:T(128)} %get-tuple-element.127, bf16[2048,258]{1,0:T(8,128)(2,1)} %get-tuple-element.138, s32[2048]{0:T(1024)S(1)} %broadcast_subtract_fusion.2, f32[256]{0:T(256)S(1)} %broadcast_maximum_fusion.2), kind=kOutput, calls=%fused_computation.8.clone.1 | convolution fusion | flops 271188992 | bytes 1717760 | tf_op jit(solution)/shard_map/while/body/eval_jaxpr/dot_general | solution.py:80
  132.2 0.6 dynamic_slice.6
  133.8 3.0 %fusion.50 = bf16[16,256,258]{1,2,0:T(8,128)(2,1)} fusion(bf16[16,256,258]{1,2,0:T(8,128)(2,1)} %get-tuple-element.128, s32[]{:T(128)} %get-tuple-element.127, bf16[2048,258]{1,0:T(8,128)(2,1)} %get-tuple-element.138, s32[2048]{0:T(1024)S(1)} %broadcast_subtract_fusion.2, f32[256]{0:T(256)S(1)} %broadcast_maximum_fusion.2), kind=kOutput, calls=%fused_computation.8.clone.1 | convolution fusion | flops 271188992 | bytes 1717760 | tf_op jit(solution)/shard_map/while/body/eval_jaxpr/dot_general | solution.py:80
  138.4 3.0 %fusion.50 = bf16[16,256,258]{1,2,0:T(8,128)(2,1)} fusion(bf16[16,256,258]{1,2,0:T(8,128)(2,1)} %get-tuple-element.128, s32[]{:T(128)} %get-tuple-element.127, bf16[2048,258]{1,0:T(8,128)(2,1)} %get-tuple-element.138, s32[2048]{0:T(1024)S(1)} %broadcast_subtract_fusion.2, f32[256]{0:T(256)S(1)} %broadcast_maximum_fusion.2), kind=kOutput, calls=%fused_computation.8.clone.1 | convolution fusion | flops 271188992 | bytes 1717760 | tf_op jit(solution)/shard_map/while/body/eval_jaxpr/dot_general | solution.py:80
  143.1 3.1 %fusion.50 = bf16[16,256,258]{1,2,0:T(8,128)(2,1)} fusion(bf16[16,256,258]{1,2,0:T(8,128)(2,1)} %get-tuple-element.128, s32[]{:T(128)} %get-tuple-element.127, bf16[2048,258]{1,0:T(8,128)(2,1)} %get-tuple-element.138, s32[2048]{0:T(1024)S(1)} %broadcast_subtract_fusion.2, f32[256]{0:T(256)S(1)} %broadcast_maximum_fusion.2), kind=kOutput, calls=%fused_computation.8.clone.1 | convolution fusion | flops 271188992 | bytes 1717760 | tf_op jit(solution)/shard_map/while/body/eval_jaxpr/dot_general | solution.py:80
  147.7 3.1 %fusion.50 = bf16[16,256,258]{1,2,0:T(8,128)(2,1)} fusion(bf16[16,256,258]{1,2,0:T(8,128)(2,1)} %get-tuple-element.128, s32[]{:T(128)} %get-tuple-element.127, bf16[2048,258]{1,0:T(8,128)(2,1)} %get-tuple-element.138, s32[2048]{0:T(1024)S(1)} %broadcast_subtract_fusion.2, f32[256]{0:T(256)S(1)} %broadcast_maximum_fusion.2), kind=kOutput, calls=%fused_computation.8.clone.1 | convolution fusion | flops 271188992 | bytes 1717760 | tf_op jit(solution)/shard_map/while/body/eval_jaxpr/dot_general | solution.py:80
  150.8 2.1 copy.39
  152.9 73.6 %all-gather.2.cloned.1.call-done = bf16[129,2,256,128]{3,2,0,1:T(8,128)(2,1)} async-done(((bf16[129,2,16,128]{3,2,0,1:T(8,128)(2,1)}), bf16[129,2,256,128]{3,2,0,1:T(8,128)(2,1)}) %all-gather.2.cloned.1.call-update) | async-done | bytes 16908304 | tf_op jit(solution)/shard_map/all_gather | solution.py:119
  226.4 4.8 %fusion.12 = f32[129,16,128]{2,1,0:T(8,128)S(1)} fusion(bf16[129,2,256,128]{3,2,0,1:T(8,128)(2,1)} %all-gather.2.cloned.1.call-done, bf16[129,2,16,256]{3,2,0,1:T(8,128)(2,1)S(1)} %bitcast.76), kind=kOutput, calls=%fused_computation.18 | convolution fusion | flops 135266304 | bytes 10567680 | tf_op jit(solution)/shard_map/bhv,bvy->bhy/dot_general | solution.py:94
  231.2 5.4 %fusion.11 = f32[129,16,128]{2,1,0:T(8,128)S(1)} fusion(bf16[129,2,256,128]{3,2,0,1:T(8,128)(2,1)} %all-gather.2.cloned.1.call-done, bf16[129,2,16,256]{3,2,0,1:T(8,128)(2,1)S(1)} %bitcast.77), kind=kOutput, calls=%fused_computation.17 | convolution fusion | flops 135266304 | bytes 10567680 | tf_op jit(solution)/shard_map/bhv,bvy->bhy/dot_general | solution.py:94
  237.1 1.3 fusion.24
  238.4 1.3 fusion.25
  240.0 15.4 %all_to_all.16 = bf16[2,129,2,8,128]{4,3,1,2,0:T(8,128)(2,1)S(1)} all-to-all(bf16[2,129,2,8,128]{4,3,1,2,0:T(8,128)(2,1)S(1)} %copy_bitcast_fusion), channel_id=1, replica_groups=mesh['shot'=16,'rcv'=8,'surf'=2] {'surf'}, dimensions={0} | all-to-all | bytes 2113536 | tf_op jit(solution)/shard_map/all_to_all | solution.py:17
  255.8 0.9 copy.43
  (82 shorter events, 11.7 us)
Async XLA Ops:
  6.5 3.0 %copy-start = (bf16[1,1024,256]{2,1,0:T(8,128)(2,1)S(1)}, bf16[1,1024,256]{2,1,0:T(8,128)(2,1)}, u32[]{:S(2)}) copy-start(bf16[1,1024,256]{2,1,0:T(8,128)(2,1)} %param.7) | copy-start | bytes 1572868
  6.5 219.9 %all-gather.2.cloned.1.call-start = ((), (), s32[]{:S(2)}) async-start(), calls=%async_computation.3 | async-start | bytes 17965056 | tf_op jit(solution)/shard_map/all_gather | solution.py:119
  10.3 0.7 copy-start.3
  13.7 11.2 %copy-start.4 = (s32[1,1024]{1,0:T(1,128)S(1)}, s32[1,1024]{1,0:T(1,128)}, u32[]{:S(2)}) copy-start(s32[1,1024]{1,0:T(1,128)} %param.10) | copy-start | bytes 12292
  13.7 11.2 %copy-start.5 = (s32[1,1024]{1,0:T(1,128)S(1)}, s32[1,1024]{1,0:T(1,128)}, u32[]{:S(2)}) copy-start(s32[1,1024]{1,0:T(1,128)} %param.9) | copy-start | bytes 12292
  15.5 45.4 %all-to-all-start.1 = ((bf16[16,128,2,129]{1,2,3,0:T(2,128)(2,1)}), bf16[16,128,2,129]{1,2,3,0:T(2,128)(2,1)S(1)}, u32[]{:S(2)}, u32[]{:S(2)}) async-start(bf16[16,128,2,129]{1,2,3,0:T(2,128)(2,1)} %copy.36), calls=%async_computation.1 | async-start | bytes 2113536 | tf_op jit(solution)/shard_map/all_to_all | solution.py:115
  61.0 5.1 %copy-start.2 = (bf16[16,128,2,129]{1,2,3,0:T(2,128)(2,1)}, bf16[16,128,2,129]{1,2,3,0:T(2,128)(2,1)S(1)}, u32[]{:S(2)}) copy-start(bf16[16,128,2,129]{1,2,3,0:T(2,128)(2,1)S(1)} %all-to-all-done.1) | copy-start | bytes 3170308
  61.0 15.3 %all-to-all-start = ((s32[16,1,128]{2,1,0:T(1,128)}), s32[16,1,128]{2,1,0:T(1,128)S(1)}, u32[]{:S(2)}, u32[]{:S(2)}) async-start(s32[16,1,128]{2,1,0:T(1,128)} %compare_select_fusion), calls=%async_computation | async-start | bytes 16384 | tf_op jit(solution)/shard_map/all_to_all | solution.py:116
  226.4 10.6 %copy-start.1 = (bf16[129,2,256,128]{3,2,0,1:T(8,128)(2,1)S(1)}, bf16[129,2,256,128]{3,2,0,1:T(8,128)(2,1)}, u32[]{:S(2)}) copy-start(bf16[129,2,256,128]{3,2,0,1:T(8,128)(2,1)} %all-gather.2.cloned.1.call-done) | copy-start | bytes 50724868
Sparse Core Ops, SparseCore 0:
  9.1 217.2 all-gather.1
where the time goes:
time: 265 us; the launch traced here: 264 us
  waiting for transfers between devices  107 us (40%)
  matrix products  64.6 us (24%)
  local copies, waits for them, and re-layouts  28.3 us (11%)
  blocking collectives  15.4 us (6%)
  starting transfers between devices  14.5 us (5%)
  between operations  13.6 us (5%)
  loops' own time  10.6 us (4%)
  other arithmetic  9.28 us (4%)
    all_gather x1, waiting for transfers between devices, local(): receiver = lax.all_gather(recv_panel, 'shot', axis=2, tiled=True)  73.6 us
    dot_general x16, matrix products, one_shot(): lax.dot_general(point_hit.astype(jnp.bfloat16), flat_rows, (((0,), (0,)),...  48.9 us
    all_to_all x1, waiting for transfers between devices, local(): lax.all_to_all(buffer, 'shot', split_axis=0, concat_axis=0, tiled=True)  33.8 us
    all_to_all x1, blocking collectives, summed_on_arrival(): parts = lax.all_to_all(split_up(array, dim, size), axis, 0, 0, tiled=True)  15.4 us
    unnamed x17, local copies, waits for them, and re-layouts  13.8 us
    dot_general x4, matrix products, product(): jnp.einsum('bhv,bvy->bhy', left_edge, right_edge, preferred_element_type=...  12.7 us
    another operation x1, loops' own time, bin_panel(): panel = lax.map(one_shot, jnp.arange(shot_rows, dtype=jnp.int32))  10.6 us
    all_to_all x1, starting transfers between devices, local(): lax.all_to_all(buffer, 'shot', split_axis=0, concat_axis=0, tiled=True)  9.39 us
  transfers between devices with their start and end apart: 3, of which 2 were waited for; matrix products, arithmetic and copies ran while one was open for 32% of the time, Pallas kernels for 0%

commit v1 on v0

--- a/solution.py
+++ b/solution.py
@@ -5,6 +5,13 @@
 from jax.sharding import PartitionSpec as P
 
 SHOTS_PER_INDEX = 16
+
+
+def all_by_exchange(x, name, dim):
+    count = lax.axis_size(name)
+    blocks = jnp.stack([x for _ in range(count)])
+    blocks = lax.all_to_all(blocks, name, split_axis=0, concat_axis=0)
+    return jnp.concatenate(blocks, axis=dim)
 
 
 def split_up(array, dim, size):
@@ -116,7 +123,7 @@
         lax.all_to_all(labels, "shot", split_axis=0, concat_axis=0, tiled=True),
     )
     panel = bin_panel(received, got_labels, SHOTS_PER_INDEX, half_points)
-    receiver = lax.all_gather(recv_panel, "shot", axis=2, tiled=True)
+    receiver = all_by_exchange(recv_panel, "shot", 2)
     real_part = product(panel[:, 0], receiver[:, 0]) - product(panel[:, 1], receiver[:, 1])
     imag_part = product(panel[:, 0], receiver[:, 1]) + product(panel[:, 1], receiver[:, 0])
     partial_value = jnp.stack([real_part, imag_part], axis=1)

time: 265 us -> 472 us (1.78)
  the two profiles are of different devices: /device:TPU:23 before, /device:TPU:143 now
where the time goes in v1:
time: 472 us; the launch traced here: 470 us
  waiting for transfers between devices  320 us (68%)
  matrix products  57.4 us (12%)
  local copies, waits for them, and re-layouts  43.5 us (9%)
  starting transfers between devices  24 us (5%)
  other arithmetic  10.7 us (2%)
  loops' own time  10.2 us (2%)
  blocking collectives  4.72 us (1%)
    all_to_all x1, waiting for transfers between devices, all_by_exchange(): blocks = lax.all_to_all(blocks, name, split_axis=0, concat_axis=0)  298 us
    dot_general x16, matrix products, one_shot(): lax.dot_general(point_hit.astype(jnp.bfloat16), flat_rows, (((0,), (0,)),...  48.6 us
    all_to_all x1, waiting for transfers between devices, local(): lax.all_to_all(buffer, 'shot', split_axis=0, concat_axis=0, tiled=True)  21.6 us
    unnamed x11, local copies, waits for them, and re-layouts  12 us
    another operation x1, loops' own time, bin_panel(): panel = lax.map(one_shot, jnp.arange(shot_rows, dtype=jnp.int32))  10.2 us
    dynamic_slice x16, local copies, waits for them, and re-layouts, bin_panel(): panel = lax.map(one_shot, jnp.arange(shot_rows, dtype=jnp.int32))  10.2 us
    reshape x1, local copies, waits for them, and re-layouts, all_by_exchange(): return jnp.concatenate(blocks, axis=dim)  10 us
  transfers between devices with their start and end apart: 3, of which 2 were waited for; matrix products, arithmetic and copies ran while one was open for 18% of the time, Pallas kernels for 0%

profile of v1, /device:TPU:143, one launch (start us, length us, event | category | flops | bytes accessed | tf_op | source)
XLA Modules:
  0.0 470.4 jit_solution(15858669965410426840)
XLA Ops:
  0.0 1.3 fusion.27
  1.3 0.7 convert_add_fusion
  2.0 0.7 multiply_add_fusion
  2.7 1.6 select_reduce_fusion
  4.9 7.6 %all-to-all-start = ((s32[16,1,128]{2,1,0:T(1,128)}), s32[16,1,128]{2,1,0:T(1,128)S(1)}, u32[]{:S(2)}, u32[]{:S(2)}) async-start(s32[16,1,128]{2,1,0:T(1,128)} %compare_select_fusion), calls=%async_computation | async-start | bytes 16384 | tf_op jit(solution)/shard_map/all_to_all | solution.py:123
  14.0 1.8 fusion.17
  16.3 1.8 copy.39
  18.1 7.6 %all-to-all-start.1 = ((bf16[16,128,2,129]{1,2,3,0:T(2,128)(2,1)}), bf16[16,128,2,129]{1,2,3,0:T(2,128)(2,1)S(1)}, u32[]{:S(2)}, u32[]{:S(2)}) async-start(bf16[16,128,2,129]{1,2,3,0:T(2,128)(2,1)} %copy.39), calls=%async_computation.1 | async-start | bytes 2113536 | tf_op jit(solution)/shard_map/all_to_all | solution.py:122
  25.6 1.4 copy.43
  27.1 21.6 %all-to-all-done.1 = bf16[16,128,2,129]{1,2,3,0:T(2,128)(2,1)S(1)} async-done(((bf16[16,128,2,129]{1,2,3,0:T(2,128)(2,1)}), bf16[16,128,2,129]{1,2,3,0:T(2,128)(2,1)S(1)}, u32[]{:S(2)}, u32[]{:S(2)}) %all-to-all-start.1) | async-done | bytes 1056800 | tf_op jit(solution)/shard_map/all_to_all | solution.py:122
  48.7 6.2 %stack.46 = bf16[16,129,2,16,128]{4,3,1,2,0:T(8,128)(2,1)} broadcast(bf16[129,2,16,128]{3,2,0,1:T(8,128)(2,1)S(1)} %copy.43), dimensions={1,2,3,4} | broadcast | bytes 17965056 | tf_op jit(solution)/shard_map/stack | solution.py:12
  54.9 8.8 %all-to-all-start.2 = ((bf16[16,129,2,16,128]{4,3,1,2,0:T(8,128)(2,1)}), bf16[16,129,2,16,128]{4,3,1,2,0:T(8,128)(2,1)}, u32[]{:S(2)}, u32[]{:S(2)}) async-start(bf16[16,129,2,16,128]{4,3,1,2,0:T(8,128)(2,1)} %stack.46), calls=%async_computation.2 | async-start | bytes 33816576 | tf_op jit(solution)/shard_map/all_to_all | solution.py:13
  63.7 8.1 %copy.48 = bf16[16,128,2,129]{3,2,1,0:T(2,128)(2,1)S(1)} copy(bf16[16,128,2,129]{1,2,3,0:T(2,128)(2,1)} %copy-done.2) | data formatting | bytes 2113536
  71.9 2.0 reshape.88
  73.9 74.7 %while.11 = (s32[]{:T(128)}, bf16[16,256,258]{1,2,0:T(8,128)(2,1)}, s32[16]{0:T(128)S(1)}, s32[2048]{0:T(1024)S(1)}, bf16[2048,258]{1,0:T(8,128)(2,1)}, /*index=5*/s32[]{:T(128)}, s32[1]{0:T(128)}) while((s32[]{:T(128)}, bf16[16,256,258]{1,2,0:T(8,128)(2,1)}, s32[16]{0:T(128)S(1)}, s32[2048]{0:T(1024)S(1)}, ...), condition=%wide.region_4.5_spmd.clone, body=%wide.region_2.4_spmd.clone.sunk | while | flops 272763904 | bytes 1745013 | solution.py:96
  73.9 0.6 dynamic_slice.6
  75.5 3.0 fusion.50
  80.2 3.0 fusion.50
  83.2 0.6 dynamic_slice.6
  84.8 3.0 fusion.50
  87.9 0.6 dynamic_slice.6
  89.5 3.0 fusion.50
  92.5 0.6 dynamic_slice.6
  94.2 3.1 fusion.50
  98.9 3.0 fusion.50
  101.9 0.6 dynamic_slice.6
  103.5 3.0 fusion.50
  108.2 3.0 fusion.50
  111.2 0.6 dynamic_slice.6
  112.9 3.1 fusion.50
  115.9 0.6 dynamic_slice.6
  117.6 3.0 fusion.50
  120.6 0.6 dynamic_slice.6
  122.2 3.0 fusion.50
  126.9 3.0 fusion.50
  131.6 3.0 fusion.50
  136.2 3.0 fusion.50
  140.9 3.0 fusion.50
  145.6 3.0 fusion.50
  148.6 2.0 copy.42
  150.6 298.2 %all-to-all-done.2 = bf16[16,129,2,16,128]{4,3,1,2,0:T(8,128)(2,1)} async-done(((bf16[16,129,2,16,128]{4,3,1,2,0:T(8,128)(2,1)}), bf16[16,129,2,16,128]{4,3,1,2,0:T(8,128)(2,1)}, u32[]{:S(2)}, u32[]{:S(2)}) %all-to-all-start.2) | async-done | bytes 16908320 | tf_op jit(solution)/shard_map/all_to_all | solution.py:13
  448.8 10.0 %copy.44 = bf16[129,2,16,16,128]{4,3,2,0,1:T(8,128)(2,1)S(1)} copy(bf16[129,2,16,16,128]{4,3,0,1,2:T(8,128)(2,1)} %bitcast.11) | data formatting | bytes 33816576 | tf_op jit(solution)/shard_map/reshape | solution.py:14
  458.9 1.2 fusion.11
  460.1 1.2 fusion.12
  461.3 1.3 fusion.25
  462.7 1.3 fusion.24
  464.3 4.7 %all_to_all.21 = bf16[2,129,2,8,128]{4,3,1,2,0:T(8,128)(2,1)S(1)} all-to-all(bf16[2,129,2,8,128]{4,3,1,2,0:T(8,128)(2,1)S(1)} %copy_bitcast_fusion), channel_id=1, replica_groups=mesh['shot'=16,'rcv'=8,'surf'=2] {'surf'}, dimensions={0} | all-to-all | bytes 2113536 | tf_op jit(solution)/shard_map/all_to_all | solution.py:24
  469.5 0.9 copy.47
  (77 shorter events, 14.2 us)
Async XLA Ops:
  0.0 13.1 %copy-start = (bf16[1,1024,256]{2,1,0:T(8,128)(2,1)S(1)}, bf16[1,1024,256]{2,1,0:T(8,128)(2,1)}, u32[]{:S(2)}) copy-start(bf16[1,1024,256]{2,1,0:T(8,128)(2,1)} %param.7) | copy-start | bytes 1572868
  4.9 13.2 %all-to-all-start = ((s32[16,1,128]{2,1,0:T(1,128)}), s32[16,1,128]{2,1,0:T(1,128)S(1)}, u32[]{:S(2)}, u32[]{:S(2)}) async-start(s32[16,1,128]{2,1,0:T(1,128)} %compare_select_fusion), calls=%async_computation | async-start | bytes 16384 | tf_op jit(solution)/shard_map/all_to_all | solution.py:123
  18.1 30.6 %all-to-all-start.1 = ((bf16[16,128,2,129]{1,2,3,0:T(2,128)(2,1)}), bf16[16,128,2,129]{1,2,3,0:T(2,128)(2,1)S(1)}, u32[]{:S(2)}, u32[]{:S(2)}) async-start(bf16[16,128,2,129]{1,2,3,0:T(2,128)(2,1)} %copy.39), calls=%async_computation.1 | async-start | bytes 2113536 | tf_op jit(solution)/shard_map/all_to_all | solution.py:122
  48.7 6.2 %copy-start.2 = (bf16[16,128,2,129]{1,2,3,0:T(2,128)(2,1)}, bf16[16,128,2,129]{1,2,3,0:T(2,128)(2,1)S(1)}, u32[]{:S(2)}) copy-start(bf16[16,128,2,129]{1,2,3,0:T(2,128)(2,1)S(1)} %all-to-all-done.1) | copy-start | bytes 3170308
  54.9 393.9 %all-to-all-start.2 = ((bf16[16,129,2,16,128]{4,3,1,2,0:T(8,128)(2,1)}), bf16[16,129,2,16,128]{4,3,1,2,0:T(8,128)(2,1)}, u32[]{:S(2)}, u32[]{:S(2)}) async-start(bf16[16,129,2,16,128]{4,3,1,2,0:T(8,128)(2,1)} %stack.46), calls=%async_computation.2 | async-start | bytes 33816576 | tf_op jit(solution)/shard_map/all_to_all | solution.py:13
  464.1 6.3 %copy-start.1 = (bf16[1,1024,256]{2,1,0:T(8,128)(2,1)S(1)}, bf16[1,1024,256]{2,1,0:T(8,128)(2,1)}, u32[]{:S(2)}) copy-start(bf16[1,1024,256]{2,1,0:T(8,128)(2,1)} %param.7) | copy-start | bytes 1572868
